TPU v7x, 512 devices: a whole 4x8x8 slice. The times are simulated.
512 devices in a mesh: doc: 32 (over y, x), seq: 16 (over z, core).
Axes of the slice: x: 4, y: 8, z: 8, core: 2. Of those that a mesh axis runs over, the one named last changes fastest.
Arguments:
- tokens: bfloat16 [131072, 1024], P(('doc', 'seq')), parts along dimension 0, may hold values from -8 to 8
- bottom_qkv: bfloat16 [1024, 3072], P('seq'), may hold values from -1 to 1
- bottom_out: bfloat16 [1024, 1024], P('seq'), may hold values from -0.5 to 0.5
- top_qkv: bfloat16 [1024, 3, 1024], P(None, None, 'seq'), may hold values from -1 to 1
- top_out: bfloat16 [1024, 1024], P('seq'), may hold values from -0.5 to 0.5
- cross_query: bfloat16 [1024, 1024], P('seq'), may hold values from -1 to 1
- cross_kv: bfloat16 [1024, 2, 1024], P(None, None, 'seq'), may hold values from -1 to 1
- cross_out: bfloat16 [1024, 1024], P('seq'), may hold values from -0.5 to 0.5
Outputs:
- encoded: bfloat16 [131072, 1024], P(('doc', 'seq')), parts along dimension 0
There are 32 independent parts, one for each index of `doc`. A program takes and returns all parts, laid end to end along the dimension named above; an argument that names none is the same for every part. Nothing has to cross between parts.
All inputs are finite; a program needn't handle non-finite values.
Results may differ from a plain program's by a relative error of at most 0.013.
Values may be sent and summed in bfloat16 or wider, within the bound.
A program may use at most 64 MiB of HBM per device.

v0:
```python
import math
import jax
import jax.numpy as jnp
from jax import lax
from jax.sharding import PartitionSpec as P

H = 16
W = 512
POOL = 32
EPS = 1e-06


def padded(cells, sides, width):
    for axis, dim in sides:
        count = lax.axis_size(axis)
        ends = count - 1
        head = lax.slice_in_dim(cells, 0, width, axis=dim)
        tail = lax.slice_in_dim(cells, cells.shape[dim] - width, cells.shape[dim], axis=dim)
        cells = jnp.concatenate(
            [
                lax.ppermute(tail, axis, [(i, (i + 1) % count) for i in range(ends)]),
                cells,
                lax.ppermute(head, axis, [((i + 1) % count, i) for i in range(ends)]),
            ],
            axis=dim,
        )
    return cells


def normed(values_in):
    values_in = values_in.astype(jnp.float32)
    return (
        values_in * lax.rsqrt(jnp.mean(values_in * values_in, axis=-1, keepdims=True) + EPS)
    ).astype(jnp.bfloat16)


def window_mask(first_tok, tok_count, half_win, total_tok):
    query_pos = first_tok + jnp.arange(tok_count, dtype=jnp.int32)
    key_pos = first_tok - half_win + jnp.arange(tok_count + 2 * half_win, dtype=jnp.int32)
    offsets = key_pos[None, :] - query_pos[:, None]
    inside = (key_pos[None, :] >= 0) & (key_pos[None, :] < total_tok)
    return (offsets >= -half_win) & (offsets < half_win) & inside


def attend(queries, key_mat, value_mat, allowed, head_count):
    row_count = queries.shape[0]
    key_count = key_mat.shape[0]
    head_width = queries.shape[1] // head_count
    score_scale = 1.0 / math.sqrt(head_width)
    split_q = queries.reshape(row_count, head_count, head_width).transpose(1, 0, 2)
    split_k = key_mat.reshape(key_count, head_count, head_width).transpose(1, 0, 2)
    split_v = value_mat.reshape(key_count, head_count, head_width).transpose(1, 0, 2)

    def one_head(operands):
        query_h, key_h, value_h = operands
        scores = jnp.dot(query_h, key_h.T, preferred_element_type=jnp.float32) * score_scale
        if allowed is not None:
            scores = jnp.where(allowed, scores, -1e30)
        row_peak = jnp.max(scores, axis=1, keepdims=True)
        expo = jnp.exp(scores - row_peak)
        row_total = jnp.sum(expo, axis=1, keepdims=True)
        mixture = (
            jnp.dot(expo.astype(jnp.bfloat16), value_h, preferred_element_type=jnp.float32)
            / row_total
        )
        return mixture.astype(jnp.bfloat16)

    merged = lax.map(one_head, (split_q, split_k, split_v))
    return merged.transpose(1, 0, 2).reshape(row_count, head_count * head_width)


def fold_rows(operand, shard_rows):
    return jnp.dot(operand, shard_rows, preferred_element_type=jnp.float32)


def local(tokens, bottom_qkv, bottom_out, top_qkv, top_out, cross_query, cross_kv, cross_out):
    tok_count, model_width = tokens.shape
    devices_seq = lax.axis_size("seq")
    local_heads = H // devices_seq
    half_win = W // 2
    total_tok = tok_count * devices_seq
    first_tok = lax.axis_index("seq") * tok_count
    normed_tok = normed(tokens)
    project = fold_rows(normed_tok, lax.all_gather(bottom_qkv, "seq", axis=0, tiled=True))
    project = project.astype(jnp.bfloat16)
    queries = project[:, :model_width]
    key_vals = padded(project[:, model_width:], (("seq", 0),), half_win)
    allowed = window_mask(first_tok, tok_count, half_win, total_tok)
    attended = attend(queries, key_vals[:, :model_width], key_vals[:, model_width:], allowed, H)
    out_sum = fold_rows(attended, lax.all_gather(bottom_out, "seq", axis=0, tiled=True))
    lower_tok = (tokens.astype(jnp.float32) + out_sum).astype(jnp.bfloat16)
    pooled = jnp.mean(
        lower_tok.astype(jnp.float32).reshape(tok_count // POOL, POOL, model_width), axis=1
    ).astype(jnp.bfloat16)
    all_units = lax.all_gather(pooled, "seq", axis=0, tiled=True)
    unit_norm = normed(all_units)
    top_q = jnp.dot(unit_norm, top_qkv[:, 0, :], preferred_element_type=jnp.float32).astype(
        jnp.bfloat16
    )
    top_k = jnp.dot(unit_norm, top_qkv[:, 1, :], preferred_element_type=jnp.float32).astype(
        jnp.bfloat16
    )
    top_v = jnp.dot(unit_norm, top_qkv[:, 2, :], preferred_element_type=jnp.float32).astype(
        jnp.bfloat16
    )
    top_att = attend(top_q, top_k, top_v, None, local_heads)
    head_term = jnp.dot(top_att, top_out, preferred_element_type=jnp.float32)
    head_total = lax.psum(head_term.astype(jnp.bfloat16), "seq").astype(jnp.float32)
    top_units = (all_units.astype(jnp.float32) + head_total).astype(jnp.bfloat16)
    upper_norm = normed(top_units)
    part_keys = jnp.dot(upper_norm, cross_kv[:, 0, :], preferred_element_type=jnp.float32).astype(
        jnp.bfloat16
    )
    part_vals = jnp.dot(upper_norm, cross_kv[:, 1, :], preferred_element_type=jnp.float32).astype(
        jnp.bfloat16
    )
    stacked = jnp.concatenate([part_keys, part_vals], axis=1)
    gathered = lax.all_gather(stacked, "seq", axis=1, tiled=True)
    unit_count = gathered.shape[0]
    arranged = gathered.reshape(unit_count, devices_seq, 2, part_keys.shape[1])
    cross_keys = arranged[:, :, 0, :].reshape(unit_count, model_width)
    cross_vals = arranged[:, :, 1, :].reshape(unit_count, model_width)
    lower_norm = normed(lower_tok)
    query_acc = fold_rows(lower_norm, lax.all_gather(cross_query, "seq", axis=0, tiled=True))
    cross_q = query_acc.astype(jnp.bfloat16)
    cross_att = attend(cross_q, cross_keys, cross_vals, None, H)
    cross_sum = fold_rows(cross_att, lax.all_gather(cross_out, "seq", axis=0, tiled=True))
    return (lower_tok.astype(jnp.float32) + cross_sum).astype(jnp.bfloat16)


def solution(mesh):
    in_specs = (
        P(("doc", "seq"), None),
        P("seq", None),
        P("seq", None),
        P(None, None, "seq"),
        P("seq", None),
        P("seq", None),
        P(None, None, "seq"),
        P("seq", None),
    )
    out_specs = P(("doc", "seq"), None)
    return jax.shard_map(local, mesh=mesh, in_specs=in_specs, out_specs=out_specs, check_vma=False)
```

profile of v0, /device:TPU:1, one launch (start us, length us, event | category | flops | bytes accessed | tf_op | source)
XLA Modules:
  0.0 322.5 jit_solution(8568578363218023782)
XLA Ops:
  9.3 55.6 %all-gather.5.cloned.1.call-done = bf16[1024,3072]{1,0:T(8,128)(2,1)} async-done(((bf16[64,3072]{1,0:T(8,128)(2,1)}), bf16[1024,3072]{1,0:T(8,128)(2,1)}) %all-gather.5.cloned.1.call-update) | async-done | bytes 6291472 | tf_op jit(solution)/shard_map/all_gather | solution.py:84
  64.9 4.8 %convolution_convert_fusion = bf16[256,3072]{1,0:T(8,128)(2,1)S(1)} fusion(bf16[1024,3072]{1,0:T(8,128)(2,1)} %all-gather.5.cloned.1.call-done, bf16[256,1024]{1,0:T(8,128)(2,1)} %param.12, f32[256]{0:T(256)S(1)} %add_rsqrt_fusion.1), kind=kOutput, calls=%fused_computation.40 | convolution fusion | flops 1612185600 | bytes 8389632 | tf_op jit(solution)/shard_map/dot_general | solution.py:73
  69.8 2.7 collective-permute-start
  72.5 2.6 collective-permute-start.1
  76.3 10.8 %collective-permute-done = bf16[256,2048]{1,0:T(8,128)(2,1)} collective-permute-done((bf16[256,2048]{1,0:T(8,128)(2,1)S(1)}, bf16[256,2048]{1,0:T(8,128)(2,1)}, u32[]{:S(2)}, u32[]{:S(2)}) %collective-permute-start) | collective-permute-done | bytes 1048608 | tf_op jit(solution)/shard_map/ppermute | solution.py:21
  87.1 6.1 %collective-permute-done.1 = bf16[256,2048]{1,0:T(8,128)(2,1)} collective-permute-done((bf16[256,2048]{1,0:T(8,128)(2,1)S(1)}, bf16[256,2048]{1,0:T(8,128)(2,1)}, u32[]{:S(2)}, u32[]{:S(2)}) %collective-permute-start.1) | collective-permute-done | bytes 1048608 | tf_op jit(solution)/shard_map/ppermute | solution.py:23
  93.2 1.7 pad_maximum_fusion
  95.2 1.6 copy.16
  97.6 33.1 %while.26 = (s32[]{:T(128)}, bf16[16,256,64]{1,2,0:T(8,128)(2,1)S(1)}, bf16[16,256,64]{1,2,0:T(8,128)(2,1)}, bf16[16,768,64]{1,2,0:T(8,128)(2,1)}, bf16[16,768,6...) while((s32[]{:T(128)}, ...), condition=%wide.region_4.5_spmd.clone, body=%wide.region_1.4_spmd.clone.sunk | while | flops 52723200 | bytes 2633565 | solution.py:68
  97.6 1.4 fusion.111
  99.7 1.4 fusion.111
  101.8 1.4 fusion.111
  103.8 1.4 fusion.111
  105.9 1.4 fusion.111
  108.0 1.4 fusion.111
  110.0 1.4 fusion.111
  112.1 1.4 fusion.111
  114.1 1.4 fusion.111
  116.2 1.4 fusion.111
  118.3 1.4 fusion.111
  120.3 1.4 fusion.111
  122.4 1.4 fusion.111
  124.5 1.4 fusion.111
  128.6 1.4 fusion.111
  130.7 2.4 bitcast_reduce_fusion
  133.1 16.1 %all_gather.21 = bf16[128,1024]{1,0:T(8,128)(2,1)S(1)} all-gather(bf16[8,1024]{1,0:T(8,128)(2,1)S(1)} %multiply_convert_fusion.2), channel_id=1, replica_groups=mesh['doc'=32,'seq'=16] {'seq'}, dimensions={0}, use_global_device_ids=true | all-gather | bytes 278528 | tf_op jit(solution)/shard_map/all_gather | solution.py:95
  152.4 2.3 convolution_convert_fusion.1
  154.9 112.5 %all-reduce.2.cloned.1.call-done = bf16[128,1024]{1,0:T(8,128)(2,1)} async-done(((bf16[128,1024]{1,0:T(8,128)(2,1)}), bf16[128,1024]{1,0:T(8,128)(2,1)}) %all-reduce.2.cloned.1.call-update) | async-done | bytes 262160 | tf_op jit(solution)/shard_map/psum | solution.py:108
  271.1 16.9 %all_gather.22 = bf16[128,2048]{0,1:T(8,128)(2,1)S(1)} all-gather(bf16[128,128]{0,1:T(8,128)(2,1)S(1)} %pad_maximum_fusion.1), channel_id=1, replica_groups=mesh['doc'=32,'seq'=16] {'seq'}, dimensions={1}, use_global_device_ids=true | all-gather | bytes 557056 | tf_op jit(solution)/shard_map/all_gather | solution.py:118
  288.7 7.1 %while.25 = (s32[]{:T(128)}, bf16[16,256,64]{1,2,0:T(8,128)(2,1)S(1)}, bf16[16,256,64]{1,2,0:T(8,128)(2,1)S(1)}, bf16[16,128,64]{2,1,0:T(8,128)(2,1)S(1)}, bf16[16,128,64]{2,1,0:T(8,128)(2,1)S(1)}, /*index=5*/s32[]{:T(128)}) while((s32[]{:T(128)}, bf16[16,256,64]{1,2,0:T(8,128)(2,1)S(1)}, bf16[16,256,64]{1,2,0:T(8,128)(2,1)S(1)}, ...), condition=%wide.region_15.16_spmd, body=%wide.region_12.15_spmd.sunk | while | flops 8617474 | bytes 531525 | solution.py:68
  295.8 17.0 %all-gather.11.cloned.1.call-done = bf16[1024,1024]{1,0:T(8,128)(2,1)} async-done(((bf16[64,1024]{1,0:T(8,128)(2,1)}), bf16[1024,1024]{1,0:T(8,128)(2,1)}) %all-gather.11.cloned.1.call-update) | async-done | bytes 2097168 | tf_op jit(solution)/shard_map/all_gather | solution.py:127
  312.8 3.1 fusion.37
  (132 shorter events, 31.2 us)
Async XLA Ops:
  6.5 144.0 %copy-start = (bf16[64,1024]{1,0:T(8,128)(2,1)S(1)}, bf16[64,1024]{1,0:T(8,128)(2,1)}, u32[]{:S(2)}) copy-start(bf16[64,1024]{1,0:T(8,128)(2,1)} %param.16) | copy-start | bytes 393220
  6.5 58.4 %all-gather.5.cloned.1.call-start = ((), (), s32[]{:S(2)}) async-start(), calls=%async_computation | async-start | bytes 6684672 | tf_op jit(solution)/shard_map/all_gather | solution.py:84
  7.3 123.4 %all-gather.7.cloned.1.call-start = ((), (), s32[]{:S(2)}) async-start(), calls=%async_computation.1 | async-start | bytes 2228224 | tf_op jit(solution)/shard_map/all_gather | solution.py:90
  8.0 144.4 %all-gather.9.cloned.1.call-start = ((), (), s32[]{:S(2)}) async-start(), calls=%async_computation.2 | async-start | bytes 2228224 | tf_op jit(solution)/shard_map/all_gather | solution.py:124
  69.8 17.2 %collective-permute-start = (bf16[256,2048]{1,0:T(8,128)(2,1)S(1)}, bf16[256,2048]{1,0:T(8,128)(2,1)}, u32[]{:S(2)}, u32[]{:S(2)}) collective-permute-start(bf16[256,2048]{1,0:T(8,128)(2,1)S(1)} %slice.45), channel_id=1, source_target_pairs={{0,1},{1,2},{2,3},{3,4},{4,5},{5,6},{6,7},{7,8},{8,9},{9,10},{10,1... | collective-permute-start | bytes 3145736 | tf_op jit(solution)/shard_map/ppermute | solution.py:21
  72.5 20.7 %collective-permute-start.1 = (bf16[256,2048]{1,0:T(8,128)(2,1)S(1)}, bf16[256,2048]{1,0:T(8,128)(2,1)}, u32[]{:S(2)}, u32[]{:S(2)}) collective-permute-start(bf16[256,2048]{1,0:T(8,128)(2,1)S(1)} %slice.45), channel_id=1, source_target_pairs={{1,0},{2,1},{3,2},{4,3},{5,4},{6,5},{7,6},{8,7},{9,8},{10,9},{11,1... | collective-permute-start | bytes 3145736 | tf_op jit(solution)/shard_map/ppermute | solution.py:23
  75.2 192.3 %all-reduce.2.cloned.1.call-start = ((), (), s32[]{:S(2)}) async-start(), calls=%async_computation.3 | async-start | bytes 524288 | tf_op jit(solution)/shard_map/psum | solution.py:108
  97.6 33.1 %copy-start.1 = (bf16[256,1024]{1,0:T(8,128)(2,1)S(1)}, bf16[256,1024]{1,0:T(8,128)(2,1)}, u32[]{:S(2)}) copy-start(bf16[256,1024]{1,0:T(8,128)(2,1)} %param.12) | copy-start | bytes 1572868
  130.7 18.7 %copy-start.2 = (bf16[1024,3,64]{0,2,1:T(8,128)(2,1)S(1)}, bf16[1024,3,64]{0,2,1:T(8,128)(2,1)}, u32[]{:S(2)}) copy-start(bf16[1024,3,64]{0,2,1:T(8,128)(2,1)} %param.15) | copy-start | bytes 1179652
  151.5 161.3 %all-gather.11.cloned.1.call-start = ((), (), s32[]{:S(2)}) async-start(), calls=%async_computation.4 | async-start | bytes 2228224 | tf_op jit(solution)/shard_map/all_gather | solution.py:127
  152.3 116.3 %copy-start.3 = (bf16[1024,2,64]{0,2,1:T(8,128)(2,1)S(1)}, bf16[1024,2,64]{0,2,1:T(8,128)(2,1)}, u32[]{:S(2)}) copy-start(bf16[1024,2,64]{0,2,1:T(8,128)(2,1)} %param.18) | copy-start | bytes 786436
Sparse Core Ops, SparseCore 0:
  9.5 55.3 all-gather.4
  67.0 41.1 all-gather.6
  110.3 42.0 all-gather.8
  154.6 112.8 all-reduce.1
  269.6 43.1 all-gather.10
where the time goes:
time: 323 us; the launch traced here: 322 us
  waiting for transfers between devices  204 us (63%)
  matrix products  51.4 us (16%)
  blocking collectives  33 us (10%)
  between operations  13.4 us (4%)
  other arithmetic  9.66 us (3%)
  starting transfers between devices  5.46 us (2%)
  local copies, waits for them, and re-layouts  4.62 us (1%)
    psum x1, waiting for transfers between devices, local(): lax.psum(head_term.astype(jnp.bfloat16), 'seq').astype(jnp.float32)  113 us
    all_gather x1, waiting for transfers between devices, local(): lax.all_gather(bottom_qkv, 'seq', axis=0, tiled=True)  55.6 us
    dot_general x33, matrix products, one_head(): jnp.dot(query_h, key_h.T, preferred_element_type=jnp.float32) * score_scale  25.3 us
    all_gather x1, waiting for transfers between devices, local(): lax.all_gather(cross_out, 'seq', axis=0, tiled=True)  17 us
    all_gather x1, blocking collectives, local(): gathered = lax.all_gather(stacked, 'seq', axis=1, tiled=True)  16.9 us
    all_gather x1, blocking collectives, local(): all_units = lax.all_gather(pooled, 'seq', axis=0, tiled=True)  16.1 us
    dot_general x4, matrix products, fold_rows(): return jnp.dot(operand, shard_rows, preferred_element_type=jnp.float32)  12.7 us
    ppermute x1, waiting for transfers between devices, padded(): lax.ppermute(tail, axis, [(i, (i + 1) % count) for i in range(ends)])  10.8 us
  transfers between devices with their start and end apart: 7, of which 6 were waited for; matrix products, arithmetic and copies ran while one was open for 19% of the time, Pallas kernels for 0%

commit v1 on v0

--- a/solution.py
+++ b/solution.py
@@ -81,7 +81,18 @@
     total_tok = tok_count * devices_seq
     first_tok = lax.axis_index("seq") * tok_count
     normed_tok = normed(tokens)
-    project = fold_rows(normed_tok, lax.all_gather(bottom_qkv, "seq", axis=0, tiled=True))
+    project = fold_rows(
+        normed_tok,
+        jnp.concatenate(
+            lax.all_to_all(
+                jnp.stack([bottom_qkv for _ in range(lax.axis_size("seq"))]),
+                axis_name="seq",
+                split_axis=0,
+                concat_axis=0,
+            ),
+            0,
+        ),
+    )
     project = project.astype(jnp.bfloat16)
     queries = project[:, :model_width]
     key_vals = padded(project[:, model_width:], (("seq", 0),), half_win)

time: 323 us -> 439 us (1.36)
  waiting for transfers between devices: 204 us -> 289 us
  matrix products: 51.4 us -> 65.4 us
  starting transfers between devices: 5.46 us -> 17.4 us
  local copies, waits for them, and re-layouts: 4.62 us -> 9.99 us
    all_to_all x0 -> x1, waiting for transfers between devices: none -> 147 us  [local(): lax.all_to_all(jnp.stack([bottom_qkv for _ in range(lax.axis_size('seq'))...]
    all_gather x1 -> x0, waiting for transfers between devices: 55.6 us -> none  [local(): lax.all_gather(bottom_qkv, 'seq', axis=0, tiled=True)]
    dot_general x33, matrix products: 9.71 us -> 24 us  [one_head(): jnp.dot(expo.astype(jnp.bfloat16), value_h, preferred_element_type=jnp.fl...]
    all_to_all x0 -> x1, starting transfers between devices: none -> 12 us  [local(): lax.all_to_all(jnp.stack([bottom_qkv for _ in range(lax.axis_size('seq'))...]
    another operation x2 -> x3, local copies, waits for them, and re-layouts: 0.1 us -> 4.58 us  [the longest x1 4.49 us: local(): jnp.stack([bottom_qkv for _ in range(lax.axis_size('seq'))])]
  transfers between devices with their start and end apart: 7 -> 7, of which waited for: 6 -> 5; matrix products, arithmetic and copies ran while one was open for 19% -> 17% of each run, Pallas kernels for 0% -> 0%
where the time goes in v1:
time: 439 us; the launch traced here: 438 us
  waiting for transfers between devices  289 us (66%)
  matrix products  65.4 us (15%)
  blocking collectives  33.4 us (8%)
  starting transfers between devices  17.4 us (4%)
  between operations  13.4 us (3%)
  local copies, waits for them, and re-layouts  9.99 us (2%)
  other arithmetic  8.6 us (2%)
    all_to_all x1, waiting for transfers between devices, local(): lax.all_to_all(jnp.stack([bottom_qkv for _ in range(lax.axis_size('seq'))...  147 us
    psum x1, waiting for transfers between devices, local(): lax.psum(head_term.astype(jnp.bfloat16), 'seq').astype(jnp.float32)  111 us
    dot_general x33, matrix products, one_head(): jnp.dot(query_h, key_h.T, preferred_element_type=jnp.float32) * score_scale  25.2 us
    dot_general x33, matrix products, one_head(): jnp.dot(expo.astype(jnp.bfloat16), value_h, preferred_element_type=jnp.fl...  24 us
    all_gather x1, waiting for transfers between devices, local(): lax.all_gather(cross_out, 'seq', axis=0, tiled=True)  17.2 us
    all_gather x1, blocking collectives, local(): gathered = lax.all_gather(stacked, 'seq', axis=1, tiled=True)  16.9 us
    all_gather x1, blocking collectives, local(): all_units = lax.all_gather(pooled, 'seq', axis=0, tiled=True)  16.4 us
    dot_general x4, matrix products, fold_rows(): return jnp.dot(operand, shard_rows, preferred_element_type=jnp.float32)  12.5 us
  transfers between devices with their start and end apart: 7, of which 5 were waited for; matrix products, arithmetic and copies ran while one was open for 17% of the time, Pallas kernels for 0%

profile of v1, /device:TPU:1, one launch (start us, length us, event | category | flops | bytes accessed | tf_op | source)
XLA Modules:
  0.0 437.8 jit_solution(11218612947903077331)
XLA Ops:
  6.5 4.5 %stack.2 = bf16[16,64,3072]{2,1,0:T(8,128)(2,1)} broadcast(bf16[64,3072]{1,0:T(8,128)(2,1)} %param.13), dimensions={1,2} | broadcast | bytes 6684672 | tf_op jit(solution)/shard_map/stack | solution.py:88
  11.0 12.0 %all-to-all-start = ((bf16[16,64,3072]{2,1,0:T(8,128)(2,1)}), bf16[16,64,3072]{2,1,0:T(8,128)(2,1)}, u32[]{:S(2)}, u32[]{:S(2)}) async-start(bf16[16,64,3072]{2,1,0:T(8,128)(2,1)} %stack.2), calls=%async_computation | async-start | bytes 12582912 | tf_op jit(solution)/shard_map/all_to_all | solution.py:87
  24.0 147.4 %all-to-all-done = bf16[16,64,3072]{2,1,0:T(8,128)(2,1)} async-done(((bf16[16,64,3072]{2,1,0:T(8,128)(2,1)}), bf16[16,64,3072]{2,1,0:T(8,128)(2,1)}, u32[]{:S(2)}, u32[]{:S(2)}) %all-to-all-start) | async-done | bytes 6291488 | tf_op jit(solution)/shard_map/all_to_all | solution.py:87
  171.4 4.7 %convolution_convert_fusion = bf16[256,3072]{1,0:T(8,128)(2,1)S(1)} fusion(bf16[1024,3072]{1,0:T(8,128)(2,1)} %bitcast.4, bf16[256,1024]{1,0:T(8,128)(2,1)S(1)} %copy-done.1, f32[256]{0:T(256)S(1)} %add_rsqrt_fusion.1), kind=kOutput, calls=%fused_computation.40 | convolution fusion | flops 1612185600 | bytes 8389632 | tf_op jit(solution)/shard_map/dot_general | solution.py:73
  176.1 2.4 collective-permute-start
  178.5 2.9 collective-permute-start.1
  182.6 7.6 %collective-permute-done = bf16[256,2048]{1,0:T(8,128)(2,1)} collective-permute-done((bf16[256,2048]{1,0:T(8,128)(2,1)S(1)}, bf16[256,2048]{1,0:T(8,128)(2,1)}, u32[]{:S(2)}, u32[]{:S(2)}) %collective-permute-start) | collective-permute-done | bytes 1048608 | tf_op jit(solution)/shard_map/ppermute | solution.py:21
  190.2 4.5 %collective-permute-done.1 = bf16[256,2048]{1,0:T(8,128)(2,1)} collective-permute-done((bf16[256,2048]{1,0:T(8,128)(2,1)S(1)}, bf16[256,2048]{1,0:T(8,128)(2,1)}, u32[]{:S(2)}, u32[]{:S(2)}) %collective-permute-start.1) | collective-permute-done | bytes 1048608 | tf_op jit(solution)/shard_map/ppermute | solution.py:23
  194.7 1.7 pad_maximum_fusion
  196.7 1.6 copy.17
  198.3 1.6 copy.16
  199.9 47.4 %while.26 = (s32[]{:T(128)}, bf16[16,256,64]{1,2,0:T(8,128)(2,1)S(1)}, bf16[16,256,64]{1,2,0:T(8,128)(2,1)}, bf16[16,768,64]{1,2,0:T(8,128)(2,1)}, bf16[16,768,6...) while((s32[]{:T(128)}, ...), condition=%wide.region_4.5_spmd.clone, body=%wide.region_1.4_spmd.clone.sunk | while | flops 52723200 | bytes 2633565 | solution.py:68
  200.0 1.4 fusion.111
  203.0 1.4 fusion.111
  205.9 1.4 fusion.111
  208.9 1.4 fusion.111
  211.8 1.4 fusion.111
  214.8 1.4 fusion.111
  220.7 1.4 fusion.111
  223.7 1.4 fusion.111
  226.6 1.4 fusion.111
  229.6 1.4 fusion.111
  232.5 1.4 fusion.111
  238.5 1.4 fusion.111
  247.4 2.4 bitcast_reduce_fusion
  249.8 16.4 %all_gather.17 = bf16[128,1024]{1,0:T(8,128)(2,1)S(1)} all-gather(bf16[8,1024]{1,0:T(8,128)(2,1)S(1)} %multiply_convert_fusion.2), channel_id=1, replica_groups=mesh['doc'=32,'seq'=16] {'seq'}, dimensions={0}, use_global_device_ids=true | all-gather | bytes 278528 | tf_op jit(solution)/shard_map/all_gather | solution.py:106
  269.3 2.4 convolution_convert_fusion.1
  271.9 110.9 %all-reduce.2.cloned.1.call-done = bf16[128,1024]{1,0:T(8,128)(2,1)} async-done(((bf16[128,1024]{1,0:T(8,128)(2,1)}), bf16[128,1024]{1,0:T(8,128)(2,1)}) %all-reduce.2.cloned.1.call-update) | async-done | bytes 262160 | tf_op jit(solution)/shard_map/psum | solution.py:119
  386.4 16.9 %all_gather.18 = bf16[128,2048]{0,1:T(8,128)(2,1)S(1)} all-gather(bf16[128,128]{0,1:T(8,128)(2,1)S(1)} %pad_maximum_fusion.1), channel_id=1, replica_groups=mesh['doc'=32,'seq'=16] {'seq'}, dimensions={1}, use_global_device_ids=true | all-gather | bytes 557056 | tf_op jit(solution)/shard_map/all_gather | solution.py:129
  404.0 7.0 %while.25 = (s32[]{:T(128)}, bf16[16,256,64]{1,2,0:T(8,128)(2,1)S(1)}, bf16[16,256,64]{1,2,0:T(8,128)(2,1)S(1)}, bf16[16,128,64]{2,1,0:T(8,128)(2,1)S(1)}, bf16[16,128,64]{2,1,0:T(8,128)(2,1)S(1)}, /*index=5*/s32[]{:T(128)}) while((s32[]{:T(128)}, bf16[16,256,64]{1,2,0:T(8,128)(2,1)S(1)}, bf16[16,256,64]{1,2,0:T(8,128)(2,1)S(1)}, ...), condition=%wide.region_15.16_spmd, body=%wide.region_12.15_spmd.sunk | while | flops 8617474 | bytes 531525 | solution.py:68
  411.0 17.2 %all-gather.8.cloned.1.call-done = bf16[1024,1024]{1,0:T(8,128)(2,1)} async-done(((bf16[64,1024]{1,0:T(8,128)(2,1)}), bf16[1024,1024]{1,0:T(8,128)(2,1)}) %all-gather.8.cloned.1.call-update) | async-done | bytes 2097168 | tf_op jit(solution)/shard_map/all_gather | solution.py:138
  428.2 3.1 fusion.37
  (134 shorter events, 46.9 us)
Async XLA Ops:
  6.5 261.1 %copy-start = (bf16[64,1024]{1,0:T(8,128)(2,1)S(1)}, bf16[64,1024]{1,0:T(8,128)(2,1)}, u32[]{:S(2)}) copy-start(bf16[64,1024]{1,0:T(8,128)(2,1)} %param.16) | copy-start | bytes 393220
  11.0 12.7 %copy-start.1 = (bf16[256,1024]{1,0:T(8,128)(2,1)S(1)}, bf16[256,1024]{1,0:T(8,128)(2,1)}, u32[]{:S(2)}) copy-start(bf16[256,1024]{1,0:T(8,128)(2,1)} %param.12) | copy-start | bytes 1572868
  11.0 160.3 %all-to-all-start = ((bf16[16,64,3072]{2,1,0:T(8,128)(2,1)}), bf16[16,64,3072]{2,1,0:T(8,128)(2,1)}, u32[]{:S(2)}, u32[]{:S(2)}) async-start(bf16[16,64,3072]{2,1,0:T(8,128)(2,1)} %stack.2), calls=%async_computation | async-start | bytes 12582912 | tf_op jit(solution)/shard_map/all_to_all | solution.py:87
  23.0 224.3 %all-gather.4.cloned.1.call-start = ((), (), s32[]{:S(2)}) async-start(), calls=%async_computation.1 | async-start | bytes 2228224 | tf_op jit(solution)/shard_map/all_gather | solution.py:101
  23.7 245.6 %all-gather.6.cloned.1.call-start = ((), (), s32[]{:S(2)}) async-start(), calls=%async_computation.2 | async-start | bytes 2228224 | tf_op jit(solution)/shard_map/all_gather | solution.py:135
  176.1 14.1 %collective-permute-start = (bf16[256,2048]{1,0:T(8,128)(2,1)S(1)}, bf16[256,2048]{1,0:T(8,128)(2,1)}, u32[]{:S(2)}, u32[]{:S(2)}) collective-permute-start(bf16[256,2048]{1,0:T(8,128)(2,1)S(1)} %slice.45), channel_id=1, source_target_pairs={{0,1},{1,2},{2,3},{3,4},{4,5},{5,6},{6,7},{7,8},{8,9},{9,10},{10,1... | collective-permute-start | bytes 3145736 | tf_op jit(solution)/shard_map/ppermute | solution.py:21
  178.5 16.2 %collective-permute-start.1 = (bf16[256,2048]{1,0:T(8,128)(2,1)S(1)}, bf16[256,2048]{1,0:T(8,128)(2,1)}, u32[]{:S(2)}, u32[]{:S(2)}) collective-permute-start(bf16[256,2048]{1,0:T(8,128)(2,1)S(1)} %slice.45), channel_id=1, source_target_pairs={{1,0},{2,1},{3,2},{4,3},{5,4},{6,5},{7,6},{8,7},{9,8},{10,9},{11,1... | collective-permute-start | bytes 3145736 | tf_op jit(solution)/shard_map/ppermute | solution.py:23
  181.4 201.3 %all-reduce.2.cloned.1.call-start = ((), (), s32[]{:S(2)}) async-start(), calls=%async_computation.3 | async-start | bytes 524288 | tf_op jit(solution)/shard_map/psum | solution.py:119
  199.9 47.4 %copy-start.2 = (bf16[256,1024]{1,0:T(8,128)(2,1)S(1)}, bf16[256,1024]{1,0:T(8,128)(2,1)}, u32[]{:S(2)}) copy-start(bf16[256,1024]{1,0:T(8,128)(2,1)} %param.12) | copy-start | bytes 1572868
  247.4 19.0 %copy-start.3 = (bf16[1024,3,64]{0,2,1:T(8,128)(2,1)S(1)}, bf16[1024,3,64]{0,2,1:T(8,128)(2,1)}, u32[]{:S(2)}) copy-start(bf16[1024,3,64]{0,2,1:T(8,128)(2,1)} %param.15) | copy-start | bytes 1179652
  268.5 159.7 %all-gather.8.cloned.1.call-start = ((), (), s32[]{:S(2)}) async-start(), calls=%async_computation.4 | async-start | bytes 2228224 | tf_op jit(solution)/shard_map/all_gather | solution.py:138
  269.3 114.6 %copy-start.4 = (bf16[1024,2,64]{0,2,1:T(8,128)(2,1)S(1)}, bf16[1024,2,64]{0,2,1:T(8,128)(2,1)}, u32[]{:S(2)}) copy-start(bf16[1024,2,64]{0,2,1:T(8,128)(2,1)} %param.18) | copy-start | bytes 786436
Sparse Core Ops, SparseCore 0:
  25.9 73.6 all-gather.3
  181.6 44.1 all-gather.5
  268.7 114.0 all-reduce.1
  385.0 43.1 all-gather.7
